TPU v7x, 32 devices: a whole 2x2x4 slice. The times are simulated.
32 devices in a mesh: seq: 8 (over y, x, core), head: 4 (over z).
Axes of the slice: x: 2, y: 2, z: 4, core: 2. Of those that a mesh axis runs over, the one named last changes fastest.
Arguments:
- queries: bfloat16 [8192, 8192], P(('seq', 'head')), may hold values from -64 to 64
- key_rows: bfloat16 [8192, 1024], P(('seq', 'head')), may hold values from -6 to 6
- value_projection_rows: bfloat16 [8192, 1024], P(('seq', 'head')), may hold values from -6 to 6
- upstream: bfloat16 [8192, 8192], P(('seq', 'head')), may hold values from -6 to 6
- ancestors: int32 [128, 2], P('seq'), may hold values from -1 to 126, as said below
Outputs:
- attended: bfloat16 [8192, 8192], P(('seq', 'head'))
- query_grad: bfloat16 [8192, 8192], P(('seq', 'head'))
- key_grad: bfloat16 [8192, 1024], P(('seq', 'head'))
- value_grad: bfloat16 [8192, 1024], P(('seq', 'head'))
Inputs may be any that keep to these rules, and one draw needn't show every extreme that they name: `ancestors`: each entry of row b is -1 (no ancestor) or a block index from max(1, b - 32) to b - 1; where that range is not empty the first entry is b - 1, and where b is a multiple of 16 the last entry is the lowest index of that range. Entries of a row may repeat.
All inputs are finite; a program needn't handle non-finite values.
Results may differ from a plain program's by a relative error of at most 0.012.
The roundings to bfloat16 on the way count: a program that leaves them out, or rounds other values in their place, can miss the bound.
Values may be sent and summed in bfloat16 or wider, within the bound.
A program may use at most 192 MiB of HBM per device.

v0:
```python
import jax
import jax.numpy as jnp
from jax import lax
from jax.sharding import PartitionSpec as P

HEAD_SIZE = 128
MASK_BLOCK_SIZE = 64
ROOT = 64
ANC = 2
NEGATIVE = -1e30


def passed_along(x, axis, by):
    length = lax.axis_size(axis)
    pairs = [(i, i + by) for i in range(length) if 0 <= i + by < length]
    return lax.ppermute(x, axis, pairs)


def from_root(x, axis, root):
    mine = lax.axis_index(axis) == root
    return lax.psum(jnp.where(mine, x, jnp.zeros_like(x)), axis)


def block_scores(query_blocks, key_heads, shared):
    if shared:
        return jnp.einsum(
            "bqkgd,skd->bkgqs", query_blocks, key_heads, preferred_element_type=jnp.float32
        )
    return jnp.einsum(
        "bqkgd,bskd->bkgqs", query_blocks, key_heads, preferred_element_type=jnp.float32
    )


def block_apply(weights, rows_heads, shared):
    if shared:
        return jnp.einsum(
            "bkgqs,skd->bqkgd", weights, rows_heads, preferred_element_type=jnp.float32
        )
    return jnp.einsum("bkgqs,bskd->bqkgd", weights, rows_heads, preferred_element_type=jnp.float32)


def block_back(weights, query_side, shared):
    if shared:
        return jnp.einsum(
            "bkgqs,bqkgd->skd", weights, query_side, preferred_element_type=jnp.float32
        )
    return jnp.einsum("bkgqs,bqkgd->bskd", weights, query_side, preferred_element_type=jnp.float32)


def local(queries, key_rows, value_projection_rows, upstream, ancestors):
    local_query, local_key, local_value = (
        lax.all_to_all(queries, "head", split_axis=1, concat_axis=0, tiled=True),
        lax.all_to_all(key_rows, "head", split_axis=1, concat_axis=0, tiled=True),
        lax.all_to_all(value_projection_rows, "head", split_axis=1, concat_axis=0, tiled=True),
    )
    tokens = local_query.shape[0]
    nblocks = tokens // MASK_BLOCK_SIZE
    kv_width = local_key.shape[1]
    kv_heads = kv_width // HEAD_SIZE
    query_groups = local_query.shape[1] // HEAD_SIZE // kv_heads
    scale = HEAD_SIZE ** (-0.5)
    shard = lax.axis_index("seq")
    near_key, near_value = passed_along((local_key, local_value), "seq", 1)
    far_key, far_value = passed_along((local_key, local_value), "seq", 2)
    tree_root_key, tree_root_value = (
        from_root(local_key[:ROOT], "seq", 0),
        from_root(local_value[:ROOT], "seq", 0),
    )
    window_key = jnp.concatenate([far_key, near_key, local_key], 0).reshape(
        3 * nblocks, MASK_BLOCK_SIZE, kv_width
    )
    window_value = jnp.concatenate([far_value, near_value, local_value], 0).reshape(
        3 * nblocks, MASK_BLOCK_SIZE, kv_width
    )
    order = jnp.arange(ANC, dtype=jnp.int32)
    before = order[None, :] < order[:, None]
    repeated = jnp.any((ancestors[:, :, None] == ancestors[:, None, :]) & before[None], axis=2)
    valid = (ancestors >= 0) & jnp.logical_not(repeated)
    relative = jnp.clip(ancestors - (shard - 2) * nblocks, 0, 3 * nblocks - 1).reshape(-1)
    ancestor_key = jnp.take(window_key, relative, axis=0).reshape(
        nblocks, ANC * MASK_BLOCK_SIZE, kv_heads, HEAD_SIZE
    )
    ancestor_value = jnp.take(window_value, relative, axis=0).reshape(
        nblocks, ANC * MASK_BLOCK_SIZE, kv_heads, HEAD_SIZE
    )
    query_pos = (shard * tokens + jnp.arange(tokens, dtype=jnp.int32)).reshape(
        nblocks, MASK_BLOCK_SIZE
    )
    root_pos = jnp.arange(ROOT, dtype=jnp.int32)
    root_mask = root_pos[None, None, :] <= query_pos[:, :, None]
    own_mask = (query_pos[:, None, :] <= query_pos[:, :, None]) & (query_pos[:, None, :] >= ROOT)
    anc_mask = jnp.broadcast_to(
        jnp.repeat(valid, MASK_BLOCK_SIZE, axis=1)[:, None, :],
        (nblocks, MASK_BLOCK_SIZE, ANC * MASK_BLOCK_SIZE),
    )
    sections = [
        (
            tree_root_key.reshape(ROOT, kv_heads, HEAD_SIZE),
            tree_root_value.reshape(ROOT, kv_heads, HEAD_SIZE),
            root_mask,
            True,
        ),
        (
            local_key.reshape(nblocks, MASK_BLOCK_SIZE, kv_heads, HEAD_SIZE),
            local_value.reshape(nblocks, MASK_BLOCK_SIZE, kv_heads, HEAD_SIZE),
            own_mask,
            False,
        ),
        (ancestor_key, ancestor_value, anc_mask, False),
    ]
    query_blocks = local_query.reshape(nblocks, MASK_BLOCK_SIZE, kv_heads, query_groups, HEAD_SIZE)
    masked_list = []
    row_max = jnp.full((nblocks, kv_heads, query_groups, MASK_BLOCK_SIZE), NEGATIVE, jnp.float32)
    row_sum = jnp.zeros((nblocks, kv_heads, query_groups, MASK_BLOCK_SIZE), jnp.float32)
    for entry in sections:
        wide_mask = entry[2][:, None, None]
        masked = jnp.where(
            wide_mask, block_scores(query_blocks, entry[0], entry[3]) * scale, NEGATIVE
        )
        sect_max = jnp.max(masked, axis=-1)
        sect_sum = jnp.sum(
            jnp.where(wide_mask, jnp.exp(masked - sect_max[..., None]), 0.0), axis=-1
        )
        new_max = jnp.maximum(row_max, sect_max)
        row_sum = row_sum * jnp.exp(row_max - new_max) + sect_sum * jnp.exp(sect_max - new_max)
        row_max = new_max
        masked_list.append(masked)
    lse = (row_max + jnp.log(row_sum))[..., None]
    prob_list = []
    out_sum = jnp.zeros((nblocks, MASK_BLOCK_SIZE, kv_heads, query_groups, HEAD_SIZE), jnp.float32)
    for number in range(3):
        entry = sections[number]
        probs = jnp.where(entry[2][:, None, None], jnp.exp(masked_list[number] - lse), 0.0).astype(
            jnp.bfloat16
        )
        prob_list.append(probs)
        out_sum = out_sum + block_apply(probs, entry[1], entry[3])
    attended_heads = lax.optimization_barrier(out_sum.astype(jnp.bfloat16))
    attended = lax.all_to_all(
        attended_heads.reshape(tokens, -1), "head", split_axis=0, concat_axis=1, tiled=True
    )
    local_upstream = lax.all_to_all(upstream, "head", split_axis=1, concat_axis=0, tiled=True)
    upstream_blocks = local_upstream.reshape(
        nblocks, MASK_BLOCK_SIZE, kv_heads, query_groups, HEAD_SIZE
    )
    delta = jnp.sum(
        upstream_blocks.astype(jnp.float32) * attended_heads.astype(jnp.float32), axis=-1
    ).transpose(0, 2, 3, 1)[..., None]
    query_sum = jnp.zeros(
        (nblocks, MASK_BLOCK_SIZE, kv_heads, query_groups, HEAD_SIZE), jnp.float32
    )
    key_parts = []
    value_parts = []
    for number in range(3):
        entry = sections[number]
        probs = prob_list[number]
        dprob = block_scores(upstream_blocks, entry[1], entry[3])
        dscore = (probs.astype(jnp.float32) * (dprob - delta)).astype(jnp.bfloat16)
        query_sum = query_sum + block_apply(dscore, entry[0], entry[3])
        key_parts.append(scale * block_back(dscore, query_blocks, entry[3]))
        value_parts.append(block_back(probs, upstream_blocks, entry[3]))
    root_key_grad, root_value_grad = lax.psum(
        (key_parts[0].reshape(ROOT, kv_width), value_parts[0].reshape(ROOT, kv_width)), "seq"
    )
    own_key = key_parts[1].reshape(tokens, kv_width)
    own_value = value_parts[1].reshape(tokens, kv_width)
    anc_both = jnp.concatenate(
        [
            key_parts[2].reshape(nblocks * ANC, MASK_BLOCK_SIZE * kv_width),
            value_parts[2].reshape(nblocks * ANC, MASK_BLOCK_SIZE * kv_width),
        ],
        1,
    )
    placing = (jnp.arange(3 * nblocks, dtype=jnp.int32)[:, None] == relative[None, :]).astype(
        jnp.float32
    )
    window_both = jnp.dot(
        placing, anc_both, precision=lax.Precision.HIGHEST, preferred_element_type=jnp.float32
    )
    window_grad_key = window_both[:, : MASK_BLOCK_SIZE * kv_width].reshape(3 * tokens, kv_width)
    window_grad_value = window_both[:, MASK_BLOCK_SIZE * kv_width :].reshape(3 * tokens, kv_width)
    far_key_grad, far_value_grad = (window_grad_key[:tokens], window_grad_value[:tokens])
    near_key_grad, near_value_grad = (
        window_grad_key[tokens : 2 * tokens],
        window_grad_value[tokens : 2 * tokens],
    )
    self_key_grad, self_value_grad = (
        window_grad_key[2 * tokens :],
        window_grad_value[2 * tokens :],
    )
    one_key, one_value = passed_along((near_key_grad, near_value_grad), "seq", -1)
    two_key, two_value = (
        passed_along(far_key_grad.astype(jnp.bfloat16), "seq", -2).astype(far_key_grad.dtype),
        passed_along(far_value_grad.astype(jnp.bfloat16), "seq", -2).astype(far_value_grad.dtype),
    )
    back_key = one_key + two_key
    back_value = one_value + two_value
    first_shard = shard == 0
    root_key_full = jnp.zeros((tokens, kv_width), jnp.float32).at[:ROOT].set(root_key_grad)
    root_value_full = jnp.zeros((tokens, kv_width), jnp.float32).at[:ROOT].set(root_value_grad)
    key_total = own_key + self_key_grad + back_key + jnp.where(first_shard, root_key_full, 0.0)
    value_total = (
        own_value + self_value_grad + back_value + jnp.where(first_shard, root_value_full, 0.0)
    )
    query_local = (scale * query_sum).astype(jnp.bfloat16).reshape(tokens, -1)
    query_grad, key_grad, value_grad = (
        lax.all_to_all(query_local, "head", split_axis=0, concat_axis=1, tiled=True),
        lax.all_to_all(
            key_total.astype(jnp.bfloat16), "head", split_axis=0, concat_axis=1, tiled=True
        ),
        lax.all_to_all(
            value_total.astype(jnp.bfloat16), "head", split_axis=0, concat_axis=1, tiled=True
        ),
    )
    return (attended, query_grad, key_grad, value_grad)


def solution(mesh):
    placed = (
        P(("seq", "head"), None),
        P(("seq", "head"), None),
        P(("seq", "head"), None),
        P(("seq", "head"), None),
        P("seq", None),
    )
    return jax.shard_map(
        local,
        mesh=mesh,
        in_specs=placed,
        out_specs=(
            P(("seq", "head"), None),
            P(("seq", "head"), None),
            P(("seq", "head"), None),
            P(("seq", "head"), None),
        ),
        check_vma=False,
    )
```

profile of v0, /device:TPU:0, one launch (start us, length us, event | category | flops | bytes accessed | tf_op | source)
XLA Modules:
  0.0 652.3 jit_solution(6052750993636207971)
XLA Ops:
  9.0 6.3 all-to-all-start.1
  17.2 12.6 %all-to-all-done.1 = bf16[256,4,256]{2,0,1:T(8,128)(2,1)S(1)} async-done(((bf16[256,4,256]{2,0,1:T(8,128)(2,1)}), bf16[256,4,256]{2,0,1:T(8,128)(2,1)S(1)}, u32[]{:S(2)}, u32[]{:S(2)}) %all-to-all-start.1) | async-done | bytes 524320 | tf_op jit(solution)/shard_map/all_to_all | solution.py:53
  29.8 3.5 all-to-all-start
  33.3 4.8 copy.506
  38.1 9.2 %all-to-all-done = bf16[256,4,256]{2,0,1:T(8,128)(2,1)S(1)} async-done(((bf16[256,4,256]{2,0,1:T(8,128)(2,1)}), bf16[256,4,256]{2,0,1:T(8,128)(2,1)S(1)}, u32[]{:S(2)}, u32[]{:S(2)}) %all-to-all-start) | async-done | bytes 524320 | tf_op jit(solution)/shard_map/all_to_all | solution.py:54
  47.3 5.0 all-to-all-start.2
  52.9 4.7 copy.505
  58.7 3.4 collective-permute-start
  62.2 2.1 collective-permute-start.1
  64.3 4.0 collective-permute-start.2
  68.3 4.0 collective-permute-start.3
  78.4 7.6 %collective-permute-done.2 = bf16[1024,256]{1,0:T(8,128)(2,1)} collective-permute-done((bf16[1024,256]{1,0:T(8,128)(2,1)S(1)}, bf16[1024,256]{1,0:T(8,128)(2,1)}, u32[]{:S(2)}, u32[]{:S(2)}) %collective-permute-start.2) | collective-permute-done | bytes 524320 | tf_op jit(solution)/shard_map/ppermute | solution.py:16
  92.9 52.1 %all-to-all-done.2 = bf16[256,4,2048]{2,0,1:T(8,128)(2,1)} async-done(((bf16[256,4,2048]{2,0,1:T(8,128)(2,1)}), bf16[256,4,2048]{2,0,1:T(8,128)(2,1)}, u32[]{:S(2)}, u32[]{:S(2)}) %all-to-all-start.2) | async-done | bytes 4194336 | tf_op jit(solution)/shard_map/all_to_all | solution.py:52
  145.0 4.8 all-to-all-start.4
  149.9 5.7 copy.384
  155.6 8.5 %bitcast_reduce_fusion = (f32[16,2,8,64]{3,2,1,0:T(8,128)}, f32[16,2,128,64,8]{2,3,4,1,0:T(8,128)}) fusion(pred[16,128]{1,0:T(8,128)(4,1)S(1)} %broadcast_in_dim_reshape.2, bf16[16,64,2,8,128]{4,3,2,1,0:T(8,128)(2,1)} %bitcast.91, bf16[16,128,2,128,1]{3,2,1,0,4:T(2,128)(2,1)S(1)} %bitcast.263), kind=kOutput, calls=%fused_computation.20 | convolution fusion | flops 543145984 | bytes 13699072 | tf_op jit(solution)/shard_map/bqkgd,bskd->bkgqs/dot_general | solution.py:29
  164.1 6.4 fusion.15
  170.5 2.9 select_reduce_fusion.1
  173.4 6.1 fusion.16
  179.6 2.9 select_reduce_fusion
  182.5 4.7 fusion.11
  187.4 4.2 select_convert_fusion
  191.7 5.5 fusion.127
  197.1 5.1 fusion.14
  202.3 4.6 fusion.31
  206.9 9.6 %fusion.8 = bf16[16,64,2,8,128]{4,1,3,0,2:T(8,128)(2,1)} fusion(f32[16,2,128,8,64]{2,4,3,0,1:T(8,128)} %fusion.31, f32[2,128,16,8,64]{1,4,3,2,0:T(8,128)} %fusion.127, bf16[16,2,8,64,64]{3,4,2,0,1:T(8,128)(2,1)S(1)} %get-tuple-element.55, bf16[16,64,2,128,1]{3,2,1,0,4:T(2,128)(2,1)S(1)} %bitcast.255), kind=kOutput, calls=%fused_computation.16 | convolution fusion | flops 274726912 | bytes 23592960 | tf_op jit(solution)/shard_map/bkgqs,bskd->bqkgd/dot_general | solution.py:39
  216.5 26.0 %all-to-all-done.4 = bf16[256,4,2048]{2,0,1:T(8,128)(2,1)} async-done(((bf16[256,4,2048]{2,0,1:T(8,128)(2,1)}), bf16[256,4,2048]{2,0,1:T(8,128)(2,1)}, u32[]{:S(2)}, u32[]{:S(2)}) %all-to-all-start.4) | async-done | bytes 4194336 | tf_op jit(solution)/shard_map/all_to_all | solution.py:142
  242.5 3.7 copy.385
  246.3 3.3 fusion.53
  250.7 2.4 multiply_reduce_fusion
  253.2 6.7 %fusion.3 = bf16[16,2,8,64,128]{4,3,2,1,0:T(8,128)(2,1)} fusion(bf16[16,2,8,64,128]{4,3,2,1,0:T(8,128)(2,1)} %copy-done.6, bf16[16,64,2,8,128]{4,3,2,1,0:T(8,128)(2,1)S(1)} %bitcast.230, bf16[16,128,2,128,1]{3,2,1,0,4:T(2,128)(2,1)S(1)} %bitcast.242, f32[16,64,2,8]{1,3,0,2:T(8,128)S(1)} %multiply_reduce_fusion), kind=kOutput, calls=%fused_computation.7 | convolution fusion | flops 545259520 | bytes 13697024 | tf_op jit(solution)/shard_map/bqkgd,bskd->bkgqs/dot_general | solution.py:29
  259.9 7.8 %fusion.5 = bf16[16,2,8,64,64]{3,4,2,0,1:T(8,128)(2,1)} fusion(bf16[16,2,8,64,64]{3,4,2,0,1:T(8,128)(2,1)} %copy-done.3, f32[16,2,8,64]{3,2,0,1:T(8,128)S(1)} %bitcast.265, bf16[16,64,2,8,128]{4,3,2,1,0:T(8,128)(2,1)S(1)} %bitcast.231, bf16[16,64,2,128,1]{3,2,1,0,4:T(2,128)(2,1)S(1)} %bitcast.256), kind=kOutput, calls=%fused_computation.11 | convolution fusion | flops 272629760 | bytes 8978432 | tf_op jit(solution)/shard_map/bqkgd,bskd->bkgqs/dot_general | solution.py:29
  267.7 5.6 fusion.7
  273.3 2.6 fusion.61
  275.9 4.2 fusion.50
  281.7 2.7 reshape.256
  284.5 3.2 copy.321
  287.7 2.8 reshape.257
  290.6 5.1 fusion.136
  297.7 2.4 slice.87
  306.0 6.1 fusion.71
  314.6 5.1 fusion.91
  322.1 5.1 fusion.81
  327.4 3.1 copy.317
  331.9 3.0 copy.328
  337.0 13.6 %collective-permute-done.7 = bf16[1024,256]{1,0:T(8,128)(2,1)} collective-permute-done((bf16[1024,256]{1,0:T(8,128)(2,1)}, bf16[1024,256]{1,0:T(8,128)(2,1)}, u32[]{:S(2)}, u32[]{:S(2)}) %collective-permute-start.7) | collective-permute-done | bytes 524320 | tf_op jit(solution)/shard_map/ppermute | solution.py:16
  352.2 40.7 %all-reduce.5.cloned.1.call-done = (f32[64,256]{1,0:T(8,128)}, f32[64,256]{1,0:T(8,128)}) async-done(((f32[64,256]{1,0:T(8,128)}, f32[64,256]{1,0:T(8,128)}), (f32[64,256]{1,0:T(8,128)}, f32[64,256]{1,0:T(8,128)})) %all-reduce.5.cloned.1.call-update) | async-done | bytes 131088 | tf_op jit(solution)/shard_map/psum | solution.py:162
  394.7 4.6 all-to-all-start.6
  399.3 7.4 %fusion.129 = f32[2,128,16,8,64]{1,4,3,2,0:T(8,128)} fusion(bf16[16,2,8,64,64]{3,4,2,0,1:T(8,128)(2,1)} %fusion.7, bf16[64,2,128]{2,0,1:T(8,128)(2,1)S(1)} %copy-done.28), kind=kOutput, calls=%fused_computation.140 | convolution fusion | flops 268435456 | bytes 10518528 | tf_op jit(solution)/shard_map/bkgqs,skd->bqkgd/dot_general | solution.py:36
  406.7 4.5 fusion.29
  412.2 5.2 all-to-all-start.7
  417.3 9.0 %fusion.1 = bf16[16,64,2,8,128]{4,1,3,0,2:T(8,128)(2,1)S(1)} fusion(f32[16,2,128,8,64]{2,4,3,0,1:T(8,128)} %fusion.29, f32[2,128,16,8,64]{1,4,3,2,0:T(8,128)} %fusion.129, bf16[16,2,8,64,64]{3,4,2,0,1:T(8,128)(2,1)} %fusion.5, bf16[16,64,2,128,1]{3,2,1,0,4:T(2,128)(2,1)S(1)} %bitcast.254), kind=kOutput, calls=%fused_computation.4 | convolution fusion | flops 276824064 | bytes 23592960 | tf_op jit(solution)/shard_map/bkgqs,bskd->bqkgd/dot_general | solution.py:39
  426.4 5.6 copy.313
  432.0 7.3 %all_to_all.126 = bf16[4,256,2048]{2,1,0:T(8,128)(2,1)} reshape(bf16[16,64,2,8,128]{4,3,2,1,0:T(8,128)(2,1)} %copy.313) | data formatting | bytes 8388608 | tf_op jit(solution)/shard_map/all_to_all | solution.py:207
  439.3 5.1 all-to-all-start.5
  444.4 7.7 %copy.298 = bf16[16,64,2,8,128]{4,3,2,1,0:T(8,128)(2,1)} copy(bf16[16,64,2,8,128]{4,1,3,0,2:T(8,128)(2,1)} %fusion.8) | data formatting | bytes 8388608 | tf_op jit(solution)/shard_map/optimization_barrier | solution.py:138
  452.1 7.3 %all_to_all.119 = bf16[4,256,2048]{2,1,0:T(8,128)(2,1)} reshape(bf16[16,64,2,8,128]{4,3,2,1,0:T(8,128)(2,1)} %copy.298) | data formatting | bytes 8388608 | tf_op jit(solution)/shard_map/all_to_all | solution.py:139
  459.4 75.8 %all-to-all-done.5 = bf16[4,256,2048]{2,1,0:T(8,128)(2,1)} async-done(((bf16[4,256,2048]{2,1,0:T(8,128)(2,1)}), bf16[4,256,2048]{2,1,0:T(8,128)(2,1)}, u32[]{:S(2)}, u32[]{:S(2)}) %all-to-all-start.5) | async-done | bytes 4194336 | tf_op jit(solution)/shard_map/all_to_all | solution.py:207
  535.2 4.9 all-to-all-start.3
  541.8 6.2 copy.314
  548.0 6.3 copy.334
  554.3 78.4 %all-to-all-done.3 = bf16[4,256,2048]{2,1,0:T(8,128)(2,1)} async-done(((bf16[4,256,2048]{2,1,0:T(8,128)(2,1)}), bf16[4,256,2048]{2,1,0:T(8,128)(2,1)}, u32[]{:S(2)}, u32[]{:S(2)}) %all-to-all-start.3) | async-done | bytes 4194336 | tf_op jit(solution)/shard_map/all_to_all | solution.py:139
  632.7 6.2 copy.299
  638.9 6.3 copy.333
  (130 shorter events, 44.0 us)
Async XLA Ops:
  9.0 20.8 %all-to-all-start.1 = ((bf16[256,4,256]{2,0,1:T(8,128)(2,1)}), bf16[256,4,256]{2,0,1:T(8,128)(2,1)S(1)}, u32[]{:S(2)}, u32[]{:S(2)}) async-start(bf16[256,4,256]{2,0,1:T(8,128)(2,1)} %bitcast.224), calls=%async_computation.1 | async-start | bytes 1048576 | tf_op jit(solution)/shard_map/all_to_all | solution.py:53
  29.8 17.4 %all-to-all-start = ((bf16[256,4,256]{2,0,1:T(8,128)(2,1)}), bf16[256,4,256]{2,0,1:T(8,128)(2,1)S(1)}, u32[]{:S(2)}, u32[]{:S(2)}) async-start(bf16[256,4,256]{2,0,1:T(8,128)(2,1)} %bitcast.225), calls=%async_computation | async-start | bytes 1048576 | tf_op jit(solution)/shard_map/all_to_all | solution.py:54
  47.3 5.1 copy-start.30
  47.3 97.7 %all-to-all-start.2 = ((bf16[256,4,2048]{2,0,1:T(8,128)(2,1)}), bf16[256,4,2048]{2,0,1:T(8,128)(2,1)}, u32[]{:S(2)}, u32[]{:S(2)}) async-start(bf16[256,4,2048]{2,0,1:T(8,128)(2,1)} %bitcast.238), calls=%async_computation.2 | async-start | bytes 8388608 | tf_op jit(solution)/shard_map/all_to_all | solution.py:52
  52.3 111.8 %all-reduce.7.cloned.1.call-start = ((), (), s32[]{:S(2)}) async-start(), calls=%async_computation.9 | async-start | bytes 131072 | tf_op jit(solution)/shard_map/psum | solution.py:21
  58.7 111.8 %copy-start.23 = (pred[16,64,64]{1,2,0:T(8,128)(4,1)}, pred[16,64,64]{1,2,0:T(8,128)(4,1)S(1)}, u32[]{:S(2)}) copy-start(pred[16,64,64]{1,2,0:T(8,128)(4,1)S(1)} %get-tuple-element.58) | copy-start | bytes 196612
  58.7 15.9 %collective-permute-start = (bf16[1024,256]{1,0:T(8,128)(2,1)S(1)}, bf16[1024,256]{1,0:T(8,128)(2,1)S(1)}, u32[]{:S(2)}, u32[]{:S(2)}) collective-permute-start(bf16[1024,256]{1,0:T(8,128)(2,1)S(1)} %bitcast.248), channel_id=1, source_target_pairs={{0,8},{4,12},{8,16},{12,20},{16,24},{20,28},{1,9},{5,13},{9,17},{1... | collective-permute-start | bytes 1572872 | tf_op jit(solution)/shard_map/ppermute | solution.py:16
  62.2 13.3 %collective-permute-start.1 = (bf16[1024,256]{1,0:T(8,128)(2,1)S(1)}, bf16[1024,256]{1,0:T(8,128)(2,1)}, u32[]{:S(2)}, u32[]{:S(2)}) collective-permute-start(bf16[1024,256]{1,0:T(8,128)(2,1)S(1)} %bitcast.249), channel_id=1, source_target_pairs={{0,4},{4,8},{8,12},{12,16},{16,20},{20,24},{24,28},{1,5},{5,9},{9,... | collective-permute-start | bytes 1572872 | tf_op jit(solution)/shard_map/ppermute | solution.py:16
  64.3 21.7 %collective-permute-start.2 = (bf16[1024,256]{1,0:T(8,128)(2,1)S(1)}, bf16[1024,256]{1,0:T(8,128)(2,1)}, u32[]{:S(2)}, u32[]{:S(2)}) collective-permute-start(bf16[1024,256]{1,0:T(8,128)(2,1)S(1)} %bitcast.243), channel_id=1, source_target_pairs={{0,8},{4,12},{8,16},{12,20},{16,24},{20,28},{1,9},{5,13},{9,17},{1... | collective-permute-start | bytes 1572872 | tf_op jit(solution)/shard_map/ppermute | solution.py:16
  68.3 17.7 %collective-permute-start.3 = (bf16[1024,256]{1,0:T(8,128)(2,1)S(1)}, bf16[1024,256]{1,0:T(8,128)(2,1)}, u32[]{:S(2)}, u32[]{:S(2)}) collective-permute-start(bf16[1024,256]{1,0:T(8,128)(2,1)S(1)} %bitcast.244), channel_id=1, source_target_pairs={{0,4},{4,8},{8,12},{12,16},{16,20},{20,24},{24,28},{1,5},{5,9},{9,... | collective-permute-start | bytes 1572872 | tf_op jit(solution)/shard_map/ppermute | solution.py:16
  72.4 101.0 %copy-start.12 = (bf16[16,64,2,128]{3,2,1,0:T(2,128)(2,1)}, bf16[16,64,2,128]{3,2,1,0:T(2,128)(2,1)S(1)}, u32[]{:S(2)}) copy-start(bf16[16,64,2,128]{3,2,1,0:T(2,128)(2,1)S(1)} %reshape.247) | copy-start | bytes 1572868
  74.7 0.8 copy-start.27
  145.0 97.5 %all-to-all-start.4 = ((bf16[256,4,2048]{2,0,1:T(8,128)(2,1)}), bf16[256,4,2048]{2,0,1:T(8,128)(2,1)}, u32[]{:S(2)}, u32[]{:S(2)}) async-start(bf16[256,4,2048]{2,0,1:T(8,128)(2,1)} %bitcast.237), calls=%async_computation.4 | async-start | bytes 8388608 | tf_op jit(solution)/shard_map/all_to_all | solution.py:142
  149.8 243.1 %all-reduce.5.cloned.1.call-start = ((), (), s32[]{:S(2)}) async-start(), calls=%async_computation.8 | async-start | bytes 262144 | tf_op jit(solution)/shard_map/psum | solution.py:162
  149.9 5.7 copy-start.16
  170.5 2.9 copy-start.21
  170.5 11.9 %slice-start = ((s8[8388608]{0:T(1024)(128)(4,1)}), s8[4194304]{0:T(1024)(128)(4,1)S(1)}, s32[]{:S(2)}) async-start(s8[8388608]{0:T(1024)(128)(4,1)} %bitcast.235), calls=%async_computation.10 | async-start | bytes 8388608
  173.4 9.0 %slice-start.1 = ((s8[8388608]{0:T(1024)(128)(4,1)}), s8[4194304]{0:T(1024)(128)(4,1)S(1)}, s32[]{:S(2)}) async-start(s8[8388608]{0:T(1024)(128)(4,1)} %bitcast.235), calls=%async_computation.11 | async-start | bytes 8388608
  179.5 2.9 copy-start.26
  182.5 4.9 copy-start.22
  182.5 4.9 copy-start.24
  187.4 4.3 copy-start.29
  191.6 5.5 copy-start.1
  191.7 15.2 %copy-start.3 = (bf16[16,2,8,64,64]{3,4,2,0,1:T(8,128)(2,1)}, bf16[16,2,8,64,64]{3,4,2,0,1:T(8,128)(2,1)S(1)}, u32[]{:S(2)}) copy-start(bf16[16,2,8,64,64]{3,4,2,0,1:T(8,128)(2,1)S(1)} %get-tuple-element.55) | copy-start | bytes 6291460
  197.1 5.1 copy-start.10
  202.2 4.6 copy-start.6
  202.3 4.6 copy-start.14
  242.5 3.8 copy-start.7
  246.3 27.1 %copy-start = (bf16[128,8,16,128]{3,2,1,0:T(8,128)(2,1)}, bf16[128,8,16,128]{3,2,1,0:T(8,128)(2,1)S(1)}, u32[]{:S(2)}) copy-start(bf16[128,8,16,128]{3,2,1,0:T(8,128)(2,1)S(1)} %copy.385) | copy-start | bytes 12582916
  246.3 4.5 copy-start.5
  250.7 2.4 copy-start.11
  259.9 7.8 %copy-start.2 = (bf16[16,2,8,64,64]{3,4,2,0,1:T(8,128)(2,1)S(1)}, bf16[16,2,8,64,64]{3,4,2,0,1:T(8,128)(2,1)}, u32[]{:S(2)}) copy-start(bf16[16,2,8,64,64]{3,4,2,0,1:T(8,128)(2,1)} %copy-done.1) | copy-start | bytes 6291460
  267.7 5.6 copy-start.4
  273.3 2.6 copy-start.8
  300.1 34.9 %collective-permute-start.4 = (f32[1024,256]{1,0:T(8,128)}, f32[1024,256]{1,0:T(8,128)}, u32[]{:S(2)}, u32[]{:S(2)}) collective-permute-start(f32[1024,256]{1,0:T(8,128)} %slice.87), channel_id=1, source_target_pairs={{4,0},{8,4},{12,8},{16,12},{20,16},{24,20},{28,24},{5,1},{9,5},{13... | collective-permute-start | bytes 3145736 | tf_op jit(solution)/shard_map/ppermute | solution.py:16
  304.5 7.5 %copy-start.20 = (f32[16,16384]{1,0:T(8,128)S(1)}, f32[16,16384]{1,0:T(8,128)}, u32[]{:S(2)}) copy-start(f32[16,16384]{1,0:T(8,128)} %get-tuple-element.49) | copy-start | bytes 3145732
  304.5 30.4 %collective-permute-start.5 = (bf16[1024,256]{1,0:T(8,128)(2,1)}, bf16[1024,256]{1,0:T(8,128)(2,1)}, u32[]{:S(2)}, u32[]{:S(2)}) collective-permute-start(bf16[1024,256]{1,0:T(8,128)(2,1)} %convert_element_type.73), channel_id=1, source_target_pairs={{8,0},{12,4},{16,8},{20,12},{24,16},{28,20},{9,1},{13,5},{17,9},{2... | collective-permute-start | bytes 1572872 | tf_op jit(solution)/shard_map/ppermute | solution.py:16
  313.2 6.5 copy-start.25
  313.2 37.4 %collective-permute-start.6 = (f32[1024,256]{1,0:T(8,128)}, f32[1024,256]{1,0:T(8,128)}, u32[]{:S(2)}, u32[]{:S(2)}) collective-permute-start(f32[1024,256]{1,0:T(8,128)} %slice.92), channel_id=1, source_target_pairs={{4,0},{8,4},{12,8},{16,12},{20,16},{24,20},{28,24},{5,1},{9,5},{13... | collective-permute-start | bytes 3145736 | tf_op jit(solution)/shard_map/ppermute | solution.py:16
  320.7 6.5 copy-start.19
  320.7 29.9 %collective-permute-start.7 = (bf16[1024,256]{1,0:T(8,128)(2,1)}, bf16[1024,256]{1,0:T(8,128)(2,1)}, u32[]{:S(2)}, u32[]{:S(2)}) collective-permute-start(bf16[1024,256]{1,0:T(8,128)(2,1)} %convert_element_type.76), channel_id=1, source_target_pairs={{8,0},{12,4},{16,8},{20,12},{24,16},{28,20},{9,1},{13,5},{17,9},{2... | collective-permute-start | bytes 1572872 | tf_op jit(solution)/shard_map/ppermute | solution.py:16
  327.2 4.6 copy-start.18
  335.0 15.6 %copy-start.15 = (f32[16,64,2,128]{3,2,1,0:T(2,128)S(1)}, f32[16,64,2,128]{3,2,1,0:T(2,128)}, u32[]{:S(2)}) copy-start(f32[16,64,2,128]{3,2,1,0:T(2,128)} %copy.328) | copy-start | bytes 3145732
  337.0 62.3 %copy-start.28 = (bf16[64,2,128]{2,0,1:T(8,128)(2,1)S(1)}, bf16[64,2,128]{2,0,1:T(8,128)(2,1)}, u32[]{:S(2)}) copy-start(bf16[64,2,128]{2,0,1:T(8,128)(2,1)} %get-tuple-element.47) | copy-start | bytes 98308
  394.7 17.5 %all-to-all-start.6 = ((bf16[4,256,256]{2,1,0:T(8,128)(2,1)}), bf16[4,256,256]{2,1,0:T(8,128)(2,1)S(1)}, u32[]{:S(2)}, u32[]{:S(2)}) async-start(bf16[4,256,256]{2,1,0:T(8,128)(2,1)} %bitcast.53), calls=%async_computation.6 | async-start | bytes 1048576 | tf_op jit(solution)/shard_map/all_to_all | solution.py:208
  399.3 7.4 %copy-start.9 = (bf16[16,2,8,64,128]{4,3,2,1,0:T(8,128)(2,1)S(1)}, bf16[16,2,8,64,128]{4,3,2,1,0:T(8,128)(2,1)}, u32[]{:S(2)}) copy-start(bf16[16,2,8,64,128]{4,3,2,1,0:T(8,128)(2,1)} %fusion.3) | copy-start | bytes 12582916
  399.3 7.4 %copy-start.17 = (bf16[16,128,2,128]{3,2,1,0:T(2,128)(2,1)S(1)}, bf16[16,128,2,128]{3,2,1,0:T(2,128)(2,1)}, u32[]{:S(2)}) copy-start(bf16[16,128,2,128]{3,2,1,0:T(2,128)(2,1)} %reshape.250) | copy-start | bytes 3145732
  406.7 10.7 %copy-start.13 = (bf16[16,64,2,128]{3,2,1,0:T(2,128)(2,1)S(1)}, bf16[16,64,2,128]{3,2,1,0:T(2,128)(2,1)}, u32[]{:S(2)}) copy-start(bf16[16,64,2,128]{3,2,1,0:T(2,128)(2,1)} %copy-done.12) | copy-start | bytes 1572868
  412.2 27.1 %all-to-all-start.7 = ((bf16[4,256,256]{2,1,0:T(8,128)(2,1)}), bf16[4,256,256]{2,1,0:T(8,128)(2,1)S(1)}, u32[]{:S(2)}, u32[]{:S(2)}) async-start(bf16[4,256,256]{2,1,0:T(8,128)(2,1)} %bitcast.61), calls=%async_computation.7 | async-start | bytes 1048576 | tf_op jit(solution)/shard_map/all_to_all | solution.py:211
  439.3 95.9 %all-to-all-start.5 = ((bf16[4,256,2048]{2,1,0:T(8,128)(2,1)}), bf16[4,256,2048]{2,1,0:T(8,128)(2,1)}, u32[]{:S(2)}, u32[]{:S(2)}) async-start(bf16[4,256,2048]{2,1,0:T(8,128)(2,1)} %all_to_all.126), calls=%async_computation.5 | async-start | bytes 8388608 | tf_op jit(solution)/shard_map/all_to_all | solution.py:207
  535.2 97.5 %all-to-all-start.3 = ((bf16[4,256,2048]{2,1,0:T(8,128)(2,1)}), bf16[4,256,2048]{2,1,0:T(8,128)(2,1)}, u32[]{:S(2)}, u32[]{:S(2)}) async-start(bf16[4,256,2048]{2,1,0:T(8,128)(2,1)} %all_to_all.119), calls=%async_computation.3 | async-start | bytes 8388608 | tf_op jit(solution)/shard_map/all_to_all | solution.py:139
Sparse Core Ops, SparseCore 0:
  74.8 52.4 all-reduce.6
  335.1 57.8 all-reduce.4
where the time goes:
time: 660 us; the launch traced here: 652 us
  waiting for transfers between devices  316 us (48%)
  local copies, waits for them, and re-layouts  114 us (17%)
  matrix products  113 us (17%)
  starting transfers between devices  58.5 us (9%)
  other arithmetic  35.4 us (5%)
  between operations  14.9 us (2%)
    all_to_all x1, waiting for transfers between devices, local(): lax.all_to_all(attended_heads.reshape(tokens, -1), 'head', split_axis=0,...  78.4 us
    all_to_all x1, waiting for transfers between devices, local(): lax.all_to_all(query_local, 'head', split_axis=0, concat_axis=1, tiled=True)  75.8 us
    all_to_all x1, waiting for transfers between devices, local(): lax.all_to_all(queries, 'head', split_axis=1, concat_axis=0, tiled=True)  52.1 us
    psum x1, waiting for transfers between devices, local(): lax.psum((key_parts[0].reshape(ROOT, kv_width), value_parts[0].reshape(RO...  40.7 us
    dot_general x4, matrix products, block_scores(): jnp.einsum('bqkgd,bskd->bkgqs', query_blocks, key_heads, preferred_elemen...  29.1 us
    dot_general x4, matrix products, block_apply(): jnp.einsum('bkgqs,bskd->bqkgd', weights, rows_heads, preferred_element_ty...  27.7 us
    all_to_all x1, waiting for transfers between devices, local(): lax.all_to_all(upstream, 'head', split_axis=1, concat_axis=0, tiled=True)  26 us
    unnamed x70, local copies, waits for them, and re-layouts  24.1 us
  transfers between devices with their start and end apart: 18, of which 10 were waited for; matrix products, arithmetic and copies ran while one was open for 27% of the time, Pallas kernels for 0%

commit v1 on v0

--- a/solution.py
+++ b/solution.py
@@ -10,6 +10,12 @@
 NEGATIVE = -1e30
 
 
+def trade_parts(x, mesh_axis, split, join):
+    pieces = jnp.split(x, lax.axis_size(mesh_axis), axis=split)
+    received = lax.all_to_all(jnp.stack(pieces), mesh_axis, 0, 0)
+    return jnp.concatenate(received, axis=join)
+
+
 def passed_along(x, axis, by):
     length = lax.axis_size(axis)
     pairs = [(i, i + by) for i in range(length) if 0 <= i + by < length]
@@ -50,7 +56,7 @@
 def local(queries, key_rows, value_projection_rows, upstream, ancestors):
     local_query, local_key, local_value = (
         lax.all_to_all(queries, "head", split_axis=1, concat_axis=0, tiled=True),
-        lax.all_to_all(key_rows, "head", split_axis=1, concat_axis=0, tiled=True),
+        trade_parts(key_rows, "head", 1, 0),
         lax.all_to_all(value_projection_rows, "head", split_axis=1, concat_axis=0, tiled=True),
     )
     tokens = local_query.shape[0]

time: 660 us -> 660 us (level)
  no operation moved by 1% of the time
where the time goes in v1:
time: 660 us; the launch traced here: 653 us
  waiting for transfers between devices  316 us (48%)
  local copies, waits for them, and re-layouts  114 us (17%)
  matrix products  113 us (17%)
  starting transfers between devices  58.5 us (9%)
  other arithmetic  36.3 us (5%)
  between operations  14.9 us (2%)
    all_to_all x1, waiting for transfers between devices, local(): lax.all_to_all(attended_heads.reshape(tokens, -1), 'head', split_axis=0,...  78.4 us
    all_to_all x1, waiting for transfers between devices, local(): lax.all_to_all(query_local, 'head', split_axis=0, concat_axis=1, tiled=True)  75.8 us
    all_to_all x1, waiting for transfers between devices, local(): lax.all_to_all(queries, 'head', split_axis=1, concat_axis=0, tiled=True)  52.1 us
    psum x1, waiting for transfers between devices, local(): lax.psum((key_parts[0].reshape(ROOT, kv_width), value_parts[0].reshape(RO...  40.7 us
    dot_general x4, matrix products, block_scores(): jnp.einsum('bqkgd,bskd->bkgqs', query_blocks, key_heads, preferred_elemen...  29.1 us
    dot_general x4, matrix products, block_apply(): jnp.einsum('bkgqs,bskd->bqkgd', weights, rows_heads, preferred_element_ty...  27.7 us
    all_to_all x1, waiting for transfers between devices, local(): lax.all_to_all(upstream, 'head', split_axis=1, concat_axis=0, tiled=True)  26 us
    unnamed x70, local copies, waits for them, and re-layouts  24.2 us
  transfers between devices with their start and end apart: 18, of which 10 were waited for; matrix products, arithmetic and copies ran while one was open for 27% of the time, Pallas kernels for 0%

profile of v1, /device:TPU:0, one launch (start us, length us, event | category | flops | bytes accessed | tf_op | source)
XLA Modules:
  0.0 652.5 jit_solution(18167614072458790293)
XLA Ops:
  9.2 6.3 all-to-all-start.1
  17.4 12.6 %all-to-all-done.1 = bf16[4,256,256]{2,1,0:T(8,128)(2,1)S(1)} async-done(((bf16[4,256,256]{2,1,0:T(8,128)(2,1)}), bf16[4,256,256]{2,1,0:T(8,128)(2,1)S(1)}, u32[]{:S(2)}, u32[]{:S(2)}) %all-to-all-start.1) | async-done | bytes 524320 | tf_op jit(solution)/shard_map/all_to_all | solution.py:15
  30.0 3.5 all-to-all-start
  33.5 4.8 copy.498
  38.2 9.2 %all-to-all-done = bf16[256,4,256]{2,0,1:T(8,128)(2,1)S(1)} async-done(((bf16[256,4,256]{2,0,1:T(8,128)(2,1)}), bf16[256,4,256]{2,0,1:T(8,128)(2,1)S(1)}, u32[]{:S(2)}, u32[]{:S(2)}) %all-to-all-start) | async-done | bytes 524320 | tf_op jit(solution)/shard_map/all_to_all | solution.py:60
  47.4 5.0 all-to-all-start.2
  53.1 4.7 copy.497
  58.9 3.4 collective-permute-start
  62.3 2.1 collective-permute-start.1
  64.4 4.0 collective-permute-start.2
  68.4 4.0 collective-permute-start.3
  78.5 7.6 %collective-permute-done.2 = bf16[1024,256]{1,0:T(8,128)(2,1)} collective-permute-done((bf16[1024,256]{1,0:T(8,128)(2,1)S(1)}, bf16[1024,256]{1,0:T(8,128)(2,1)}, u32[]{:S(2)}, u32[]{:S(2)}) %collective-permute-start.2) | collective-permute-done | bytes 524320 | tf_op jit(solution)/shard_map/ppermute | solution.py:22
  93.1 52.1 %all-to-all-done.2 = bf16[256,4,2048]{2,0,1:T(8,128)(2,1)} async-done(((bf16[256,4,2048]{2,0,1:T(8,128)(2,1)}), bf16[256,4,2048]{2,0,1:T(8,128)(2,1)}, u32[]{:S(2)}, u32[]{:S(2)}) %all-to-all-start.2) | async-done | bytes 4194336 | tf_op jit(solution)/shard_map/all_to_all | solution.py:58
  145.1 4.8 all-to-all-start.4
  150.0 5.7 copy.377
  155.7 8.5 %bitcast_reduce_fusion = (f32[16,2,8,64]{3,2,1,0:T(8,128)}, f32[16,2,128,64,8]{2,3,4,1,0:T(8,128)}) fusion(pred[16,128]{1,0:T(8,128)(4,1)S(1)} %broadcast_in_dim_reshape.2, bf16[16,64,2,8,128]{4,3,2,1,0:T(8,128)(2,1)} %bitcast.91, bf16[16,128,2,128,1]{3,2,1,0,4:T(2,128)(2,1)S(1)} %bitcast.264), kind=kOutput, calls=%fused_computation.20 | convolution fusion | flops 543145984 | bytes 13699072 | tf_op jit(solution)/shard_map/bqkgd,bskd->bkgqs/dot_general | solution.py:35
  164.2 6.4 fusion.15
  170.7 2.9 select_reduce_fusion.1
  173.6 6.1 fusion.16
  179.7 2.9 select_reduce_fusion
  182.6 4.7 fusion.11
  187.5 4.2 select_convert_fusion
  191.8 5.5 fusion.127
  197.3 5.1 fusion.14
  202.4 4.6 fusion.31
  207.0 9.6 %fusion.8 = bf16[16,64,2,8,128]{4,1,3,0,2:T(8,128)(2,1)} fusion(f32[16,2,128,8,64]{2,4,3,0,1:T(8,128)} %fusion.31, f32[2,128,16,8,64]{1,4,3,2,0:T(8,128)} %fusion.127, bf16[16,2,8,64,64]{3,4,2,0,1:T(8,128)(2,1)S(1)} %get-tuple-element.59, bf16[16,64,2,128,1]{3,2,1,0,4:T(2,128)(2,1)S(1)} %bitcast.256), kind=kOutput, calls=%fused_computation.16 | convolution fusion | flops 274726912 | bytes 23592960 | tf_op jit(solution)/shard_map/bkgqs,bskd->bqkgd/dot_general | solution.py:45
  216.6 26.0 %all-to-all-done.4 = bf16[256,4,2048]{2,0,1:T(8,128)(2,1)} async-done(((bf16[256,4,2048]{2,0,1:T(8,128)(2,1)}), bf16[256,4,2048]{2,0,1:T(8,128)(2,1)}, u32[]{:S(2)}, u32[]{:S(2)}) %all-to-all-start.4) | async-done | bytes 4194336 | tf_op jit(solution)/shard_map/all_to_all | solution.py:148
  242.6 3.7 copy.378
  246.4 3.3 fusion.53
  250.9 2.4 multiply_reduce_fusion
  253.3 6.7 %fusion.3 = bf16[16,2,8,64,128]{4,3,2,1,0:T(8,128)(2,1)} fusion(bf16[16,2,8,64,128]{4,3,2,1,0:T(8,128)(2,1)} %copy-done.6, bf16[16,64,2,8,128]{4,3,2,1,0:T(8,128)(2,1)S(1)} %bitcast.232, bf16[16,128,2,128,1]{3,2,1,0,4:T(2,128)(2,1)S(1)} %bitcast.244, f32[16,64,2,8]{1,3,0,2:T(8,128)S(1)} %multiply_reduce_fusion), kind=kOutput, calls=%fused_computation.7 | convolution fusion | flops 545259520 | bytes 13697024 | tf_op jit(solution)/shard_map/bqkgd,bskd->bkgqs/dot_general | solution.py:35
  260.0 7.8 %fusion.5 = bf16[16,2,8,64,64]{3,4,2,0,1:T(8,128)(2,1)} fusion(bf16[16,2,8,64,64]{3,4,2,0,1:T(8,128)(2,1)} %copy-done.3, f32[16,2,8,64]{3,2,0,1:T(8,128)S(1)} %bitcast.266, bf16[16,64,2,8,128]{4,3,2,1,0:T(8,128)(2,1)S(1)} %bitcast.233, bf16[16,64,2,128,1]{3,2,1,0,4:T(2,128)(2,1)S(1)} %bitcast.257), kind=kOutput, calls=%fused_computation.11 | convolution fusion | flops 272629760 | bytes 8978432 | tf_op jit(solution)/shard_map/bqkgd,bskd->bkgqs/dot_general | solution.py:35
  267.8 5.6 fusion.7
  273.5 2.6 fusion.61
  276.1 4.2 fusion.50
  281.9 2.7 reshape.252
  284.6 3.2 copy.315
  287.8 2.8 reshape.253
  290.7 5.1 fusion.136
  297.9 2.4 slice.87
  306.1 6.1 fusion.71
  314.8 5.1 fusion.91
  322.3 5.1 fusion.81
  327.5 3.1 copy.311
  332.1 3.0 copy.322
  337.2 13.5 %collective-permute-done.7 = bf16[1024,256]{1,0:T(8,128)(2,1)} collective-permute-done((bf16[1024,256]{1,0:T(8,128)(2,1)}, bf16[1024,256]{1,0:T(8,128)(2,1)}, u32[]{:S(2)}, u32[]{:S(2)}) %collective-permute-start.7) | collective-permute-done | bytes 524320 | tf_op jit(solution)/shard_map/ppermute | solution.py:22
  352.4 40.7 %all-reduce.5.cloned.1.call-done = (f32[64,256]{1,0:T(8,128)}, f32[64,256]{1,0:T(8,128)}) async-done(((f32[64,256]{1,0:T(8,128)}, f32[64,256]{1,0:T(8,128)}), (f32[64,256]{1,0:T(8,128)}, f32[64,256]{1,0:T(8,128)})) %all-reduce.5.cloned.1.call-update) | async-done | bytes 131088 | tf_op jit(solution)/shard_map/psum | solution.py:168
  394.9 4.6 all-to-all-start.6
  399.5 7.4 %fusion.129 = f32[2,128,16,8,64]{1,4,3,2,0:T(8,128)} fusion(bf16[16,2,8,64,64]{3,4,2,0,1:T(8,128)(2,1)} %fusion.7, bf16[64,2,128]{2,0,1:T(8,128)(2,1)S(1)} %copy-done.28), kind=kOutput, calls=%fused_computation.144 | convolution fusion | flops 268435456 | bytes 10518528 | tf_op jit(solution)/shard_map/bkgqs,skd->bqkgd/dot_general | solution.py:42
  406.9 4.5 fusion.29
  412.3 5.2 all-to-all-start.7
  417.5 9.0 %fusion.1 = bf16[16,64,2,8,128]{4,1,3,0,2:T(8,128)(2,1)S(1)} fusion(f32[16,2,128,8,64]{2,4,3,0,1:T(8,128)} %fusion.29, f32[2,128,16,8,64]{1,4,3,2,0:T(8,128)} %fusion.129, bf16[16,2,8,64,64]{3,4,2,0,1:T(8,128)(2,1)} %fusion.5, bf16[16,64,2,128,1]{3,2,1,0,4:T(2,128)(2,1)S(1)} %bitcast.255), kind=kOutput, calls=%fused_computation.4 | convolution fusion | flops 276824064 | bytes 23592960 | tf_op jit(solution)/shard_map/bkgqs,bskd->bqkgd/dot_general | solution.py:45
  426.6 5.6 copy.307
  432.2 7.3 %all_to_all.112 = bf16[4,256,2048]{2,1,0:T(8,128)(2,1)} reshape(bf16[16,64,2,8,128]{4,3,2,1,0:T(8,128)(2,1)} %copy.307) | data formatting | bytes 8388608 | tf_op jit(solution)/shard_map/all_to_all | solution.py:213
  439.5 5.1 all-to-all-start.5
  444.6 7.7 %copy.292 = bf16[16,64,2,8,128]{4,3,2,1,0:T(8,128)(2,1)} copy(bf16[16,64,2,8,128]{4,1,3,0,2:T(8,128)(2,1)} %fusion.8) | data formatting | bytes 8388608 | tf_op jit(solution)/shard_map/optimization_barrier | solution.py:144
  452.3 7.3 %all_to_all.105 = bf16[4,256,2048]{2,1,0:T(8,128)(2,1)} reshape(bf16[16,64,2,8,128]{4,3,2,1,0:T(8,128)(2,1)} %copy.292) | data formatting | bytes 8388608 | tf_op jit(solution)/shard_map/all_to_all | solution.py:145
  459.6 75.8 %all-to-all-done.5 = bf16[4,256,2048]{2,1,0:T(8,128)(2,1)} async-done(((bf16[4,256,2048]{2,1,0:T(8,128)(2,1)}), bf16[4,256,2048]{2,1,0:T(8,128)(2,1)}, u32[]{:S(2)}, u32[]{:S(2)}) %all-to-all-start.5) | async-done | bytes 4194336 | tf_op jit(solution)/shard_map/all_to_all | solution.py:213
  535.4 4.9 all-to-all-start.3
  542.0 6.2 copy.308
  548.2 6.3 copy.328
  554.5 78.4 %all-to-all-done.3 = bf16[4,256,2048]{2,1,0:T(8,128)(2,1)} async-done(((bf16[4,256,2048]{2,1,0:T(8,128)(2,1)}), bf16[4,256,2048]{2,1,0:T(8,128)(2,1)}, u32[]{:S(2)}, u32[]{:S(2)}) %all-to-all-start.3) | async-done | bytes 4194336 | tf_op jit(solution)/shard_map/all_to_all | solution.py:145
  632.9 6.2 copy.293
  639.1 6.3 copy.327
  (131 shorter events, 44.2 us)
Async XLA Ops:
  9.2 20.8 %all-to-all-start.1 = ((bf16[4,256,256]{2,1,0:T(8,128)(2,1)}), bf16[4,256,256]{2,1,0:T(8,128)(2,1)S(1)}, u32[]{:S(2)}, u32[]{:S(2)}) async-start(bf16[4,256,256]{2,1,0:T(8,128)(2,1)} %pad_maximum_fusion.2), calls=%async_computation.1 | async-start | bytes 1048576 | tf_op jit(solution)/shard_map/all_to_all | solution.py:15
  30.0 17.4 %all-to-all-start = ((bf16[256,4,256]{2,0,1:T(8,128)(2,1)}), bf16[256,4,256]{2,0,1:T(8,128)(2,1)S(1)}, u32[]{:S(2)}, u32[]{:S(2)}) async-start(bf16[256,4,256]{2,0,1:T(8,128)(2,1)} %bitcast.227), calls=%async_computation | async-start | bytes 1048576 | tf_op jit(solution)/shard_map/all_to_all | solution.py:60
  47.4 5.1 copy-start.30
  47.4 97.7 %all-to-all-start.2 = ((bf16[256,4,2048]{2,0,1:T(8,128)(2,1)}), bf16[256,4,2048]{2,0,1:T(8,128)(2,1)}, u32[]{:S(2)}, u32[]{:S(2)}) async-start(bf16[256,4,2048]{2,0,1:T(8,128)(2,1)} %bitcast.240), calls=%async_computation.2 | async-start | bytes 8388608 | tf_op jit(solution)/shard_map/all_to_all | solution.py:58
  52.4 111.8 %all-reduce.7.cloned.1.call-start = ((), (), s32[]{:S(2)}) async-start(), calls=%async_computation.9 | async-start | bytes 131072 | tf_op jit(solution)/shard_map/psum | solution.py:27
  58.9 111.8 %copy-start.23 = (pred[16,64,64]{1,2,0:T(8,128)(4,1)}, pred[16,64,64]{1,2,0:T(8,128)(4,1)S(1)}, u32[]{:S(2)}) copy-start(pred[16,64,64]{1,2,0:T(8,128)(4,1)S(1)} %get-tuple-element.62) | copy-start | bytes 196612
  58.9 15.9 %collective-permute-start = (bf16[1024,256]{1,0:T(8,128)(2,1)S(1)}, bf16[1024,256]{1,0:T(8,128)(2,1)S(1)}, u32[]{:S(2)}, u32[]{:S(2)}) collective-permute-start(bf16[1024,256]{1,0:T(8,128)(2,1)S(1)} %bitcast.250), channel_id=1, source_target_pairs={{0,8},{4,12},{8,16},{12,20},{16,24},{20,28},{1,9},{5,13},{9,17},{1... | collective-permute-start | bytes 1572872 | tf_op jit(solution)/shard_map/ppermute | solution.py:22
  62.3 13.3 %collective-permute-start.1 = (bf16[1024,256]{1,0:T(8,128)(2,1)S(1)}, bf16[1024,256]{1,0:T(8,128)(2,1)}, u32[]{:S(2)}, u32[]{:S(2)}) collective-permute-start(bf16[1024,256]{1,0:T(8,128)(2,1)S(1)} %bitcast.251), channel_id=1, source_target_pairs={{0,4},{4,8},{8,12},{12,16},{16,20},{20,24},{24,28},{1,5},{5,9},{9,... | collective-permute-start | bytes 1572872 | tf_op jit(solution)/shard_map/ppermute | solution.py:22
  64.4 21.7 %collective-permute-start.2 = (bf16[1024,256]{1,0:T(8,128)(2,1)S(1)}, bf16[1024,256]{1,0:T(8,128)(2,1)}, u32[]{:S(2)}, u32[]{:S(2)}) collective-permute-start(bf16[1024,256]{1,0:T(8,128)(2,1)S(1)} %bitcast.245), channel_id=1, source_target_pairs={{0,8},{4,12},{8,16},{12,20},{16,24},{20,28},{1,9},{5,13},{9,17},{1... | collective-permute-start | bytes 1572872 | tf_op jit(solution)/shard_map/ppermute | solution.py:22
  68.4 17.7 %collective-permute-start.3 = (bf16[1024,256]{1,0:T(8,128)(2,1)S(1)}, bf16[1024,256]{1,0:T(8,128)(2,1)}, u32[]{:S(2)}, u32[]{:S(2)}) collective-permute-start(bf16[1024,256]{1,0:T(8,128)(2,1)S(1)} %bitcast.246), channel_id=1, source_target_pairs={{0,4},{4,8},{8,12},{12,16},{16,20},{20,24},{24,28},{1,5},{5,9},{9,... | collective-permute-start | bytes 1572872 | tf_op jit(solution)/shard_map/ppermute | solution.py:22
  74.7 98.8 %copy-start.12 = (bf16[16,64,2,128]{3,2,1,0:T(2,128)(2,1)}, bf16[16,64,2,128]{3,2,1,0:T(2,128)(2,1)S(1)}, u32[]{:S(2)}) copy-start(bf16[16,64,2,128]{3,2,1,0:T(2,128)(2,1)S(1)} %reshape_reshape.3) | copy-start | bytes 1572868
  74.8 0.9 copy-start.27
  145.1 97.5 %all-to-all-start.4 = ((bf16[256,4,2048]{2,0,1:T(8,128)(2,1)}), bf16[256,4,2048]{2,0,1:T(8,128)(2,1)}, u32[]{:S(2)}, u32[]{:S(2)}) async-start(bf16[256,4,2048]{2,0,1:T(8,128)(2,1)} %bitcast.239), calls=%async_computation.4 | async-start | bytes 8388608 | tf_op jit(solution)/shard_map/all_to_all | solution.py:148
  150.0 243.2 %all-reduce.5.cloned.1.call-start = ((), (), s32[]{:S(2)}) async-start(), calls=%async_computation.8 | async-start | bytes 262144 | tf_op jit(solution)/shard_map/psum | solution.py:168
  150.0 5.7 copy-start.16
  170.6 2.9 copy-start.21
  170.7 11.9 %slice-start = ((s8[8388608]{0:T(1024)(128)(4,1)}), s8[4194304]{0:T(1024)(128)(4,1)S(1)}, s32[]{:S(2)}) async-start(s8[8388608]{0:T(1024)(128)(4,1)} %bitcast.237), calls=%async_computation.10 | async-start | bytes 8388608
  173.5 9.0 %slice-start.1 = ((s8[8388608]{0:T(1024)(128)(4,1)}), s8[4194304]{0:T(1024)(128)(4,1)S(1)}, s32[]{:S(2)}) async-start(s8[8388608]{0:T(1024)(128)(4,1)} %bitcast.237), calls=%async_computation.11 | async-start | bytes 8388608
  179.7 2.9 copy-start.26
  182.6 4.9 copy-start.22
  182.6 4.9 copy-start.24
  187.5 4.3 copy-start.29
  191.8 5.5 copy-start.1
  191.8 15.2 %copy-start.3 = (bf16[16,2,8,64,64]{3,4,2,0,1:T(8,128)(2,1)}, bf16[16,2,8,64,64]{3,4,2,0,1:T(8,128)(2,1)S(1)}, u32[]{:S(2)}) copy-start(bf16[16,2,8,64,64]{3,4,2,0,1:T(8,128)(2,1)S(1)} %get-tuple-element.59) | copy-start | bytes 6291460
  197.3 5.1 copy-start.10
  202.4 4.6 copy-start.6
  202.4 4.6 copy-start.14
  242.6 3.8 copy-start.7
  246.4 27.1 %copy-start = (bf16[128,8,16,128]{3,2,1,0:T(8,128)(2,1)}, bf16[128,8,16,128]{3,2,1,0:T(8,128)(2,1)S(1)}, u32[]{:S(2)}) copy-start(bf16[128,8,16,128]{3,2,1,0:T(8,128)(2,1)S(1)} %copy.378) | copy-start | bytes 12582916
  246.4 4.5 copy-start.5
  250.9 2.4 copy-start.11
  260.0 7.8 %copy-start.2 = (bf16[16,2,8,64,64]{3,4,2,0,1:T(8,128)(2,1)S(1)}, bf16[16,2,8,64,64]{3,4,2,0,1:T(8,128)(2,1)}, u32[]{:S(2)}) copy-start(bf16[16,2,8,64,64]{3,4,2,0,1:T(8,128)(2,1)} %copy-done.1) | copy-start | bytes 6291460
  267.8 5.6 copy-start.4
  273.4 2.6 copy-start.8
  300.3 34.9 %collective-permute-start.4 = (f32[1024,256]{1,0:T(8,128)}, f32[1024,256]{1,0:T(8,128)}, u32[]{:S(2)}, u32[]{:S(2)}) collective-permute-start(f32[1024,256]{1,0:T(8,128)} %slice.87), channel_id=1, source_target_pairs={{4,0},{8,4},{12,8},{16,12},{20,16},{24,20},{28,24},{5,1},{9,5},{13... | collective-permute-start | bytes 3145736 | tf_op jit(solution)/shard_map/ppermute | solution.py:22
  304.7 7.5 %copy-start.20 = (f32[16,16384]{1,0:T(8,128)S(1)}, f32[16,16384]{1,0:T(8,128)}, u32[]{:S(2)}) copy-start(f32[16,16384]{1,0:T(8,128)} %get-tuple-element.49) | copy-start | bytes 3145732
  304.7 30.5 %collective-permute-start.5 = (bf16[1024,256]{1,0:T(8,128)(2,1)}, bf16[1024,256]{1,0:T(8,128)(2,1)}, u32[]{:S(2)}, u32[]{:S(2)}) collective-permute-start(bf16[1024,256]{1,0:T(8,128)(2,1)} %convert_element_type.73), channel_id=1, source_target_pairs={{8,0},{12,4},{16,8},{20,12},{24,16},{28,20},{9,1},{13,5},{17,9},{2... | collective-permute-start | bytes 1572872 | tf_op jit(solution)/shard_map/ppermute | solution.py:22
  313.3 6.5 copy-start.25
  313.3 37.4 %collective-permute-start.6 = (f32[1024,256]{1,0:T(8,128)}, f32[1024,256]{1,0:T(8,128)}, u32[]{:S(2)}, u32[]{:S(2)}) collective-permute-start(f32[1024,256]{1,0:T(8,128)} %slice.92), channel_id=1, source_target_pairs={{4,0},{8,4},{12,8},{16,12},{20,16},{24,20},{28,24},{5,1},{9,5},{13... | collective-permute-start | bytes 3145736 | tf_op jit(solution)/shard_map/ppermute | solution.py:22
  320.9 6.5 copy-start.19
  320.9 29.8 %collective-permute-start.7 = (bf16[1024,256]{1,0:T(8,128)(2,1)}, bf16[1024,256]{1,0:T(8,128)(2,1)}, u32[]{:S(2)}, u32[]{:S(2)}) collective-permute-start(bf16[1024,256]{1,0:T(8,128)(2,1)} %convert_element_type.76), channel_id=1, source_target_pairs={{8,0},{12,4},{16,8},{20,12},{24,16},{28,20},{9,1},{13,5},{17,9},{2... | collective-permute-start | bytes 1572872 | tf_op jit(solution)/shard_map/ppermute | solution.py:22
  327.3 4.6 copy-start.18
  335.1 15.6 %copy-start.15 = (f32[16,64,2,128]{3,2,1,0:T(2,128)S(1)}, f32[16,64,2,128]{3,2,1,0:T(2,128)}, u32[]{:S(2)}) copy-start(f32[16,64,2,128]{3,2,1,0:T(2,128)} %copy.322) | copy-start | bytes 3145732
  337.2 62.3 %copy-start.28 = (bf16[64,2,128]{2,0,1:T(8,128)(2,1)S(1)}, bf16[64,2,128]{2,0,1:T(8,128)(2,1)}, u32[]{:S(2)}) copy-start(bf16[64,2,128]{2,0,1:T(8,128)(2,1)} %get-tuple-element.47) | copy-start | bytes 98308
  394.9 17.5 %all-to-all-start.6 = ((bf16[4,256,256]{2,1,0:T(8,128)(2,1)}), bf16[4,256,256]{2,1,0:T(8,128)(2,1)S(1)}, u32[]{:S(2)}, u32[]{:S(2)}) async-start(bf16[4,256,256]{2,1,0:T(8,128)(2,1)} %bitcast.55), calls=%async_computation.6 | async-start | bytes 1048576 | tf_op jit(solution)/shard_map/all_to_all | solution.py:214
  399.5 7.4 %copy-start.9 = (bf16[16,2,8,64,128]{4,3,2,1,0:T(8,128)(2,1)S(1)}, bf16[16,2,8,64,128]{4,3,2,1,0:T(8,128)(2,1)}, u32[]{:S(2)}) copy-start(bf16[16,2,8,64,128]{4,3,2,1,0:T(8,128)(2,1)} %fusion.3) | copy-start | bytes 12582916
  399.5 7.4 %copy-start.17 = (bf16[16,128,2,128]{3,2,1,0:T(2,128)(2,1)S(1)}, bf16[16,128,2,128]{3,2,1,0:T(2,128)(2,1)}, u32[]{:S(2)}) copy-start(bf16[16,128,2,128]{3,2,1,0:T(2,128)(2,1)} %reshape.246) | copy-start | bytes 3145732
  406.9 10.7 %copy-start.13 = (bf16[16,64,2,128]{3,2,1,0:T(2,128)(2,1)S(1)}, bf16[16,64,2,128]{3,2,1,0:T(2,128)(2,1)}, u32[]{:S(2)}) copy-start(bf16[16,64,2,128]{3,2,1,0:T(2,128)(2,1)} %copy-done.12) | copy-start | bytes 1572868
  412.3 27.1 %all-to-all-start.7 = ((bf16[4,256,256]{2,1,0:T(8,128)(2,1)}), bf16[4,256,256]{2,1,0:T(8,128)(2,1)S(1)}, u32[]{:S(2)}, u32[]{:S(2)}) async-start(bf16[4,256,256]{2,1,0:T(8,128)(2,1)} %bitcast.63), calls=%async_computation.7 | async-start | bytes 1048576 | tf_op jit(solution)/shard_map/all_to_all | solution.py:217
  439.5 95.9 %all-to-all-start.5 = ((bf16[4,256,2048]{2,1,0:T(8,128)(2,1)}), bf16[4,256,2048]{2,1,0:T(8,128)(2,1)}, u32[]{:S(2)}, u32[]{:S(2)}) async-start(bf16[4,256,2048]{2,1,0:T(8,128)(2,1)} %all_to_all.112), calls=%async_computation.5 | async-start | bytes 8388608 | tf_op jit(solution)/shard_map/all_to_all | solution.py:213
  535.4 97.5 %all-to-all-start.3 = ((bf16[4,256,2048]{2,1,0:T(8,128)(2,1)}), bf16[4,256,2048]{2,1,0:T(8,128)(2,1)}, u32[]{:S(2)}, u32[]{:S(2)}) async-start(bf16[4,256,2048]{2,1,0:T(8,128)(2,1)} %all_to_all.105), calls=%async_computation.3 | async-start | bytes 8388608 | tf_op jit(solution)/shard_map/all_to_all | solution.py:145
Sparse Core Ops, SparseCore 0:
  74.7 52.4 all-reduce.6
  335.3 57.8 all-reduce.4
